TPU v7x, 32 devices: a whole 2x2x4 slice. The times are simulated.
32 devices in a mesh: dp: 4 (over y, core), ctx: 4 (over z), tsp: 2 (over x).
Axes of the slice: x: 2, y: 2, z: 4, core: 2. Of those that a mesh axis runs over, the one named last changes fastest.
Arguments:
- grad_out: bfloat16 [4, 1024, 8192], P('dp', 'ctx', 'tsp'), may hold values from -6 to 6
- attn_out: bfloat16 [4, 1024, 4096], P('dp', None, 'ctx'), may hold values from -6 to 6
- out_weight: bfloat16 [4096, 8192], P('ctx', 'tsp'), may hold values from -0.0625 to 0.0625
- query: bfloat16 [4, 1024, 4096], P('dp', 'tsp', 'ctx'), may hold values from -128 to 128
- keys: bfloat16 [4, 1024, 512], P('dp'), may hold values from -128 to 128
- values: bfloat16 [4, 1024, 512], P('dp'), may hold values from -6 to 6
- segment_ids: int32 [4, 1024], P('dp'), may hold values from 0 to 7, never falling along the last dimension, each value on 1 to 256 neighbouring positions
- tile_live: int32 [4, 8, 8], P('dp'), may hold values 0 or 1
Outputs:
- grad_query: bfloat16 [4, 1024, 4096], P('dp', 'tsp', 'ctx')
- grad_keys: bfloat16 [4, 1024, 512], P('dp', ('ctx', 'tsp'))
- grad_values: bfloat16 [4, 1024, 512], P('dp', ('ctx', 'tsp'))
- grad_weight: float32 [4096, 8192], P('ctx', 'tsp')
Inputs may be any that keep to these rules, and one draw needn't show every extreme that they name: `segment_ids`: segment numbers never fall along a row and segment 0 is the source document; each segment has 1 to 256 tokens, one exactly that many.
All inputs are finite; a program needn't handle non-finite values. No bound on the sum of `tile_live` on one device may be relied on, other than what follows from the above.
Results may differ from a plain program's by a relative error of at most 0.0058.
Values may be sent and summed in bfloat16 or wider, within the bound.
A program may use at most 128 MiB of HBM per device.

v0:
```python
import math
import jax
import jax.numpy as jnp
from jax import lax
from jax.sharding import PartitionSpec as P

HEADS = 32
KV_HEADS = 4
HEAD_DIM = 128
TILE = 128


def merge_group(tensor_in):
    row_count = tensor_in.shape[0]
    folded = tensor_in.reshape(row_count, KV_HEADS, HEADS // KV_HEADS, HEAD_DIM).sum(axis=2)
    return folded.reshape(row_count, KV_HEADS * HEAD_DIM)


def per_device(grad_out, attn_out, out_weight, query, keys, values, segment_ids, tile_live):
    score_scale = 1.0 / math.sqrt(HEAD_DIM)
    out_all = attn_out[0]
    seq_len = out_all.shape[0]
    feat_width = out_all.shape[1]
    dy_block = lax.all_gather(grad_out, "ctx", axis=1, tiled=True)[0]
    proj_rows = lax.dot_general(
        dy_block, out_weight, (((1,), (1,)), ((), ())), preferred_element_type=jnp.float32
    )
    grad_part = proj_rows
    weight_part = lax.dot_general(
        out_all, dy_block, (((0,), (0,)), ((), ())), preferred_element_type=jnp.float32
    )
    grad_part, weight_part = (grad_part, weight_part)
    grad_weight = lax.psum(weight_part, "dp")
    out_grad = lax.psum_scatter(grad_part, "tsp", scatter_dimension=0, tiled=True).astype(
        jnp.bfloat16
    )
    quarter = out_grad.shape[0]
    row_start = lax.axis_index("tsp") * quarter
    heads_dev = feat_width // HEAD_DIM
    group_size = HEADS // KV_HEADS
    head_ids = lax.axis_index("ctx") * heads_dev + jnp.arange(heads_dev, dtype=jnp.int32)
    kv_ids = head_ids // group_size
    query_pos = row_start + jnp.arange(quarter, dtype=jnp.int32)
    key_pos = jnp.arange(seq_len, dtype=jnp.int32)
    tile_count = seq_len // TILE
    tile_rows = lax.dynamic_slice_in_dim(tile_live[0], row_start // TILE, quarter // TILE, 0)
    tile_mask = (
        jnp.broadcast_to(
            tile_rows[:, None, :, None], (quarter // TILE, TILE, tile_count, TILE)
        ).reshape(quarter, seq_len)
        == 1
    )
    same_tile = query_pos[:, None] // TILE == key_pos[None, :] // TILE
    segments = segment_ids[0]
    query_seg = lax.dynamic_slice_in_dim(segments, row_start, quarter, 0)
    same_doc = (segments[None, :] == query_seg[:, None]) | (segments[None, :] == 0)
    allowed = (tile_mask | same_tile) & same_doc & (key_pos[None, :] <= query_pos[:, None])

    def split_heads(tensor_in):
        return tensor_in.reshape(tensor_in.shape[0], heads_dev, HEAD_DIM).transpose(1, 0, 2)

    query_heads = split_heads(query[0])
    grad_heads = split_heads(out_grad)
    output_heads = split_heads(lax.dynamic_slice_in_dim(out_all, row_start, quarter, 0))
    key_table = keys[0].reshape(seq_len, KV_HEADS, HEAD_DIM)
    value_table = values[0].reshape(seq_len, KV_HEADS, HEAD_DIM)

    def one_head(head_items):
        query_head, grad_head, output_head, kv_index = head_items
        key_head = lax.dynamic_index_in_dim(key_table, kv_index, 1, keepdims=False)
        value_head = lax.dynamic_index_in_dim(value_table, kv_index, 1, keepdims=False)
        scores = (
            lax.dot_general(
                query_head, key_head, (((1,), (1,)), ((), ())), preferred_element_type=jnp.float32
            )
            * score_scale
        )
        scores = jnp.where(allowed, scores, -jnp.inf)
        row_max = jnp.max(scores, axis=1, keepdims=True)
        lse = row_max + jnp.log(jnp.sum(jnp.exp(scores - row_max), axis=1, keepdims=True))
        probs_f = jnp.where(allowed, jnp.exp(scores - lse), 0.0)
        probs = probs_f.astype(jnp.bfloat16)
        value_term = lax.dot_general(
            probs, grad_head, (((0,), (0,)), ((), ())), preferred_element_type=jnp.float32
        )
        dprobs = lax.dot_general(
            grad_head, value_head, (((1,), (1,)), ((), ())), preferred_element_type=jnp.float32
        )
        delta = jnp.sum(
            grad_head.astype(jnp.float32) * output_head.astype(jnp.float32), axis=1, keepdims=True
        )
        dscores = (probs_f * (dprobs - delta)).astype(jnp.bfloat16)
        query_grad = (
            jnp.dot(dscores, key_head, preferred_element_type=jnp.float32) * score_scale
        ).astype(jnp.bfloat16)
        key_term = (
            lax.dot_general(
                dscores, query_head, (((0,), (0,)), ((), ())), preferred_element_type=jnp.float32
            )
            * score_scale
        )
        return (query_grad, key_term, value_term)

    query_grads, key_terms, value_terms = lax.map(
        one_head, (query_heads, grad_heads, output_heads, kv_ids)
    )
    grad_query = query_grads.transpose(1, 0, 2).reshape(quarter, feat_width)
    key_cols = key_terms.transpose(1, 0, 2).reshape(seq_len, feat_width)
    value_cols = value_terms.transpose(1, 0, 2).reshape(seq_len, feat_width)
    key_recv, value_recv = (
        lax.all_to_all(key_cols, "ctx", split_axis=0, concat_axis=1, tiled=True),
        lax.all_to_all(value_cols, "ctx", split_axis=0, concat_axis=1, tiled=True),
    )
    key_part, value_part = (
        lax.psum_scatter(merge_group(key_recv), "tsp", scatter_dimension=0, tiled=True),
        lax.psum_scatter(merge_group(value_recv), "tsp", scatter_dimension=0, tiled=True),
    )
    grad_keys = key_part.astype(jnp.bfloat16)[None]
    grad_values = value_part.astype(jnp.bfloat16)[None]
    return (grad_query[None], grad_keys, grad_values, grad_weight)


def solution(mesh):
    placed = (
        P("dp", "ctx", "tsp"),
        P("dp", None, "ctx"),
        P("ctx", "tsp"),
        P("dp", "tsp", "ctx"),
        P("dp", None, None),
        P("dp", None, None),
        P("dp", None),
        P("dp", None, None),
    )
    return jax.shard_map(
        per_device,
        mesh=mesh,
        in_specs=placed,
        out_specs=(
            P("dp", "tsp", "ctx"),
            P("dp", ("ctx", "tsp"), None),
            P("dp", ("ctx", "tsp"), None),
            P("ctx", "tsp"),
        ),
        check_vma=False,
    )
```

profile of v0, /device:TPU:0, one launch (start us, length us, event | category | flops | bytes accessed | tf_op | source)
XLA Modules:
  0.0 900.4 jit_solution(15618256980744114519)
XLA Ops:
  8.0 154.0 %all-gather.2.cloned.1.call-done = bf16[1,1024,4096]{2,1,0:T(8,128)(2,1)} async-done(((bf16[1,256,4096]{2,1,0:T(8,128)(2,1)}), bf16[1,1024,4096]{2,1,0:T(8,128)(2,1)}) %all-gather.2.cloned.1.call-update) | async-done | bytes 8388624 | tf_op jit(solution)/shard_map/all_gather | solution.py:24
  161.9 15.1 %fusion.38 = f32[1024,1024]{1,0:T(8,128)} fusion(bf16[1024,4096]{1,0:T(8,128)(2,1)} %param.12, bf16[1,1024,4096]{2,1,0:T(8,128)(2,1)} %all-gather.2.cloned.1.call-done), kind=kOutput, calls=%fused_computation.47 | convolution fusion | flops 8589934592 | bytes 20971520 | tf_op jit(solution)/shard_map/dot_general | solution.py:25
  177.2 1.3 copy.66
  178.5 2.4 copy.46
  182.3 2.3 copy.49
  184.7 45.1 %reduce-scatter.4.cloned.1.call-done = f32[512,1024]{1,0:T(8,128)} async-done(((f32[1024,1024]{1,0:T(8,128)}), f32[512,1024]{1,0:T(8,128)}) %reduce-scatter.4.cloned.1.call-update) | async-done | bytes 2097168 | tf_op jit(solution)/shard_map/reduce_scatter | solution.py:34
  229.7 1.7 bitcast_bitcast_fusion
  231.5 129.6 %while.15 = (s32[]{:T(128)}, bf16[8,512,128]{2,1,0:T(8,128)(2,1)}, f32[8,1024,128]{2,1,0:T(8,128)}, f32[8,1024,128]{2,1,0:T(8,128)}, bf16[8,512,128]{1,2,0:T(8,1...) while((s32[]{:T(128)}, bf16[8,512,128]{2,1,0:T(8,128)(2,1)}, ...), condition=%wide.region_5.6_spmd.clone, body=%wide.region_1.5_spmd.clone.sunk | while | flops 689437696 | bytes 16977196 | solution.py:104
  235.4 2.4 fusion.73
  238.3 2.7 multiply_convert_fusion.2
  241.1 2.1 fusion.75
  243.1 2.4 fusion.77
  245.5 2.2 fusion.76
  251.6 2.4 fusion.73
  254.5 2.7 multiply_convert_fusion.2
  257.3 2.1 fusion.75
  259.3 2.4 fusion.77
  261.8 2.2 fusion.76
  267.9 2.4 fusion.73
  270.8 2.7 multiply_convert_fusion.2
  273.5 2.1 fusion.75
  275.6 2.4 fusion.77
  278.0 2.2 fusion.76
  284.1 2.4 fusion.73
  287.0 2.7 multiply_convert_fusion.2
  289.7 2.1 fusion.75
  291.8 2.4 fusion.77
  294.1 2.2 fusion.76
  300.3 2.4 fusion.73
  303.2 2.7 multiply_convert_fusion.2
  305.9 2.1 fusion.75
  308.0 2.4 fusion.77
  310.4 2.2 fusion.76
  316.5 2.4 fusion.73
  319.4 2.7 multiply_convert_fusion.2
  322.1 2.1 fusion.75
  324.2 2.4 fusion.77
  326.5 2.2 fusion.76
  332.7 2.4 fusion.73
  335.6 2.7 multiply_convert_fusion.2
  338.3 2.1 fusion.75
  340.4 2.4 fusion.77
  342.7 2.2 fusion.76
  348.9 2.4 fusion.73
  351.7 2.7 multiply_convert_fusion.2
  354.5 2.1 fusion.75
  356.5 2.4 fusion.77
  358.9 2.2 fusion.76
  361.1 6.6 copy.58
  367.7 4.9 all_to_all.27
  372.6 4.9 all-to-all-start.1
  377.5 6.5 copy.56
  384.0 4.9 all_to_all.24
  388.9 81.9 %all-to-all-done.1 = f32[4,256,1024]{2,1,0:T(8,128)} async-done(((f32[4,256,1024]{2,1,0:T(8,128)}), f32[4,256,1024]{2,1,0:T(8,128)}, u32[]{:S(2)}, u32[]{:S(2)}) %all-to-all-start.1) | async-done | bytes 4194336 | tf_op jit(solution)/shard_map/all_to_all | solution.py:112
  470.8 4.9 all-to-all-start
  475.8 5.1 copy.70
  480.9 3.2 reduce_sum.37
  485.2 83.3 %all-to-all-done = f32[4,256,1024]{2,1,0:T(8,128)} async-done(((f32[4,256,1024]{2,1,0:T(8,128)}), f32[4,256,1024]{2,1,0:T(8,128)}, u32[]{:S(2)}, u32[]{:S(2)}) %all-to-all-start) | async-done | bytes 4194336 | tf_op jit(solution)/shard_map/all_to_all | solution.py:111
  568.5 5.2 copy.69
  573.7 3.2 reduce_sum.36
  578.0 15.0 %fusion.36 = f32[1024,4096]{1,0:T(8,128)} fusion(bf16[1,1024,4096]{2,1,0:T(8,128)(2,1)} %all-gather.2.cloned.1.call-done, bf16[1,1024,1024]{2,1,0:T(8,128)(2,1)S(1)} %copy-done), kind=kOutput, calls=%fused_computation.45 | convolution fusion | flops 8589934592 | bytes 27262976 | tf_op jit(solution)/shard_map/dot_general | solution.py:29
  593.0 1.9 copy.55
  599.7 282.5 %all-reduce.2.cloned.1.call-done = f32[1024,4096]{1,0:T(8,128)} async-done(((f32[1024,4096]{1,0:T(8,128)}), f32[1024,4096]{1,0:T(8,128)}) %all-reduce.2.cloned.1.call-update) | async-done | bytes 16777232 | tf_op jit(solution)/shard_map/psum | solution.py:33
  882.2 11.7 %copy.104 = f32[1024,4096]{1,0:T(8,128)} copy(f32[1024,4096]{1,0:T(8,128)} %all-reduce.2.cloned.1.call-done) | data formatting | bytes 33554432
  (94 shorter events, 29.3 us)
Async XLA Ops:
  7.2 169.9 %copy-start = (bf16[1,1024,1024]{2,1,0:T(8,128)(2,1)S(1)}, bf16[1,1024,1024]{2,1,0:T(8,128)(2,1)}, u32[]{:S(2)}) copy-start(bf16[1,1024,1024]{2,1,0:T(8,128)(2,1)} %param.11) | copy-start | bytes 6291460
  7.2 154.7 %all-gather.2.cloned.1.call-start = ((), (), s32[]{:S(2)}) async-start(), calls=%async_computation.5 | async-start | bytes 10485760 | tf_op jit(solution)/shard_map/all_gather | solution.py:24
  7.9 221.8 %reduce-scatter.4.cloned.1.call-start = ((), (), s32[]{:S(2)}) async-start(), calls=%async_computation.6 | async-start | bytes 6291456 | tf_op jit(solution)/shard_map/reduce_scatter | solution.py:34
  178.5 2.4 copy-start.1
  180.9 3.6 copy-start.3
  180.9 3.7 copy-start.2
  372.6 98.3 %all-to-all-start.1 = ((f32[4,256,1024]{2,1,0:T(8,128)}), f32[4,256,1024]{2,1,0:T(8,128)}, u32[]{:S(2)}, u32[]{:S(2)}) async-start(f32[4,256,1024]{2,1,0:T(8,128)} %all_to_all.27), calls=%async_computation.3 | async-start | bytes 8388608 | tf_op jit(solution)/shard_map/all_to_all | solution.py:112
  470.8 97.7 %all-to-all-start = ((f32[4,256,1024]{2,1,0:T(8,128)}), f32[4,256,1024]{2,1,0:T(8,128)}, u32[]{:S(2)}, u32[]{:S(2)}) async-start(f32[4,256,1024]{2,1,0:T(8,128)} %all_to_all.24), calls=%async_computation.1 | async-start | bytes 8388608 | tf_op jit(solution)/shard_map/all_to_all | solution.py:111
  475.8 120.4 %reduce-scatter.8.cloned.1.call-start = ((), (), s32[]{:S(2)}) async-start(), calls=%async_computation.8 | async-start | bytes 786432 | tf_op jit(solution)/shard_map/reduce_scatter | solution.py:116
  485.1 112.8 %reduce-scatter.6.cloned.1.call-start = ((), (), s32[]{:S(2)}) async-start(), calls=%async_computation.7 | async-start | bytes 786432 | tf_op jit(solution)/shard_map/reduce_scatter | solution.py:115
  578.0 304.2 %all-reduce.2.cloned.1.call-start = ((), (), s32[]{:S(2)}) async-start(), calls=%async_computation.9 | async-start | bytes 33554432 | tf_op jit(solution)/shard_map/psum | solution.py:33
Sparse Core Ops, SparseCore 0:
  9.6 152.3 all-gather.1
  177.1 52.5 reduce-scatter.3
  485.3 15.0 reduce-scatter.7
  578.1 12.7 reduce-scatter.5
  593.8 288.3 all-reduce.1
where the time goes:
time: 902 us; the launch traced here: 900 us
  waiting for transfers between devices  648 us (72%)
  matrix products  124 us (14%)
  local copies, waits for them, and re-layouts  73.7 us (8%)
  loops' own time  15.8 us (2%)
  other arithmetic  15.5 us (2%)
  between operations  13.9 us (2%)
  starting transfers between devices  10.1 us (1%)
    psum x1, waiting for transfers between devices, per_device(): grad_weight = lax.psum(weight_part, 'dp')  282 us
    all_gather x1, waiting for transfers between devices, per_device(): dy_block = lax.all_gather(grad_out, 'ctx', axis=1, tiled=True)[0]  154 us
    all_to_all x1, waiting for transfers between devices, per_device(): lax.all_to_all(key_cols, 'ctx', split_axis=0, concat_axis=1, tiled=True)  83.3 us
    all_to_all x1, waiting for transfers between devices, per_device(): lax.all_to_all(value_cols, 'ctx', split_axis=0, concat_axis=1, tiled=True)  81.9 us
    reduce_scatter x1, waiting for transfers between devices, per_device(): lax.psum_scatter(grad_part, 'tsp', scatter_dimension=0, tiled=True)  45.1 us
    unnamed x17, local copies, waits for them, and re-layouts  31 us
    dot_general x8, matrix products, one_head(): lax.dot_general(grad_head, value_head, (((1,), (1,)), ((), ())), preferre...  21.9 us
    dot_general x8, matrix products, one_head(): lax.dot_general(probs, grad_head, (((0,), (0,)), ((), ())), preferred_ele...  19.1 us
  transfers between devices with their start and end apart: 7, of which 5 were waited for; matrix products, arithmetic and copies ran while one was open for 6% of the time, Pallas kernels for 0%

commit v1 on v0

--- a/solution.py
+++ b/solution.py
@@ -30,7 +30,7 @@
         out_all, dy_block, (((0,), (0,)), ((), ())), preferred_element_type=jnp.float32
     )
     grad_part, weight_part = (grad_part, weight_part)
-    grad_weight = lax.psum(weight_part, "dp")
+    grad_weight = jnp.sum(lax.all_gather(weight_part, axis_name="dp"), axis=0)
     out_grad = lax.psum_scatter(grad_part, "tsp", scatter_dimension=0, tiled=True).astype(
         jnp.bfloat16
     )

time: 902 us -> 1020 us (1.13)
  waiting for transfers between devices: 648 us -> 751 us
  other arithmetic: 15.5 us -> 43.5 us
  local copies, waits for them, and re-layouts: 73.7 us -> 62 us
    all_gather x0 -> x1, waiting for transfers between devices: none -> 386 us  [per_device(): grad_weight = jnp.sum(lax.all_gather(weight_part, axis_name='dp'), axis=0)]
    psum x1 -> x0, waiting for transfers between devices: 282 us -> none  [per_device(): grad_weight = lax.psum(weight_part, 'dp')]
    reduce_sum x0 -> x1, other arithmetic: none -> 27.9 us  [per_device(): grad_weight = jnp.sum(lax.all_gather(weight_part, axis_name='dp'), axis=0)]
    unnamed x17 -> x16, local copies, waits for them, and re-layouts: 31 us -> 19.2 us
  transfers between devices with their start and end apart: 7 -> 7, of which waited for: 5 -> 5; matrix products, arithmetic and copies ran while one was open for 6% -> 5% of each run, Pallas kernels for 0% -> 0%
where the time goes in v1:
time: 1020 us
  waiting for transfers between devices  751 us (74%)
  matrix products  124 us (12%)
  local copies, waits for them, and re-layouts  62 us (6%)
  other arithmetic  43.5 us (4%)
  loops' own time  15.8 us (2%)
  between operations  13.9 us (1%)
    all_gather x1, waiting for transfers between devices, per_device(): grad_weight = jnp.sum(lax.all_gather(weight_part, axis_name='dp'), axis=0)  386 us
    all_gather x1, waiting for transfers between devices, per_device(): dy_block = lax.all_gather(grad_out, 'ctx', axis=1, tiled=True)[0]  154 us
    all_to_all x1, waiting for transfers between devices, per_device(): lax.all_to_all(key_cols, 'ctx', split_axis=0, concat_axis=1, tiled=True)  83.3 us
    all_to_all x1, waiting for transfers between devices, per_device(): lax.all_to_all(value_cols, 'ctx', split_axis=0, concat_axis=1, tiled=True)  81.9 us
    reduce_scatter x1, waiting for transfers between devices, per_device(): lax.psum_scatter(grad_part, 'tsp', scatter_dimension=0, tiled=True)  45.1 us
    reduce_sum x1, other arithmetic, per_device(): grad_weight = jnp.sum(lax.all_gather(weight_part, axis_name='dp'), axis=0)  27.9 us
    dot_general x8, matrix products, one_head(): lax.dot_general(grad_head, value_head, (((1,), (1,)), ((), ())), preferre...  21.9 us
  transfers between devices with their start and end apart: 7, of which 5 were waited for; matrix products, arithmetic and copies ran while one was open for 5% of the time, Pallas kernels for 0%

profile of v1, /device:TPU:0, one launch (start us, length us, event | category | flops | bytes accessed | tf_op | source)
XLA Modules:
  0.0 1020.1 jit_solution(6384269536069524548)
XLA Ops:
  8.0 154.0 %all-gather.4.cloned.1.call-done = bf16[1,1024,4096]{2,1,0:T(8,128)(2,1)} async-done(((bf16[1,256,4096]{2,1,0:T(8,128)(2,1)}), bf16[1,1024,4096]{2,1,0:T(8,128)(2,1)}) %all-gather.4.cloned.1.call-update) | async-done | bytes 8388624 | tf_op jit(solution)/shard_map/all_gather | solution.py:24
  161.9 15.1 %fusion.38 = f32[1024,1024]{1,0:T(8,128)} fusion(bf16[1024,4096]{1,0:T(8,128)(2,1)} %param.12, bf16[1,1024,4096]{2,1,0:T(8,128)(2,1)} %all-gather.4.cloned.1.call-done), kind=kOutput, calls=%fused_computation.47 | convolution fusion | flops 8589934592 | bytes 20971520 | tf_op jit(solution)/shard_map/dot_general | solution.py:25
  177.2 1.3 copy.66
  178.5 2.4 copy.46
  182.3 2.3 copy.49
  184.7 45.1 %reduce-scatter.4.cloned.1.call-done = f32[512,1024]{1,0:T(8,128)} async-done(((f32[1024,1024]{1,0:T(8,128)}), f32[512,1024]{1,0:T(8,128)}) %reduce-scatter.4.cloned.1.call-update) | async-done | bytes 2097168 | tf_op jit(solution)/shard_map/reduce_scatter | solution.py:34
  229.7 1.7 bitcast_bitcast_fusion
  231.5 129.6 %while.15 = (s32[]{:T(128)}, bf16[8,512,128]{2,1,0:T(8,128)(2,1)}, f32[8,1024,128]{2,1,0:T(8,128)}, f32[8,1024,128]{2,1,0:T(8,128)}, bf16[8,512,128]{1,2,0:T(8,1...) while((s32[]{:T(128)}, bf16[8,512,128]{2,1,0:T(8,128)(2,1)}, ...), condition=%wide.region_5.6_spmd.clone, body=%wide.region_1.5_spmd.clone.sunk | while | flops 689437696 | bytes 16977196 | solution.py:104
  235.4 2.4 fusion.73
  238.3 2.7 multiply_convert_fusion.2
  241.1 2.1 fusion.75
  243.1 2.4 fusion.77
  245.5 2.2 fusion.76
  251.6 2.4 fusion.73
  254.5 2.7 multiply_convert_fusion.2
  257.3 2.1 fusion.75
  259.3 2.4 fusion.77
  261.8 2.2 fusion.76
  267.9 2.4 fusion.73
  270.8 2.7 multiply_convert_fusion.2
  273.5 2.1 fusion.75
  275.6 2.4 fusion.77
  278.0 2.2 fusion.76
  284.1 2.4 fusion.73
  287.0 2.7 multiply_convert_fusion.2
  289.7 2.1 fusion.75
  291.8 2.4 fusion.77
  294.1 2.2 fusion.76
  300.3 2.4 fusion.73
  303.2 2.7 multiply_convert_fusion.2
  305.9 2.1 fusion.75
  308.0 2.4 fusion.77
  310.4 2.2 fusion.76
  316.5 2.4 fusion.73
  319.4 2.7 multiply_convert_fusion.2
  322.1 2.1 fusion.75
  324.2 2.4 fusion.77
  326.5 2.2 fusion.76
  332.7 2.4 fusion.73
  335.6 2.7 multiply_convert_fusion.2
  338.3 2.1 fusion.75
  340.4 2.4 fusion.77
  342.7 2.2 fusion.76
  348.9 2.4 fusion.73
  351.7 2.7 multiply_convert_fusion.2
  354.5 2.1 fusion.75
  356.5 2.4 fusion.77
  358.9 2.2 fusion.76
  361.1 6.6 copy.58
  367.7 4.9 all_to_all.27
  372.6 4.9 all-to-all-start.1
  377.5 6.5 copy.56
  384.0 4.9 all_to_all.24
  388.9 81.9 %all-to-all-done.1 = f32[4,256,1024]{2,1,0:T(8,128)} async-done(((f32[4,256,1024]{2,1,0:T(8,128)}), f32[4,256,1024]{2,1,0:T(8,128)}, u32[]{:S(2)}, u32[]{:S(2)}) %all-to-all-start.1) | async-done | bytes 4194336 | tf_op jit(solution)/shard_map/all_to_all | solution.py:112
  470.8 4.9 all-to-all-start
  475.8 5.1 copy.70
  480.9 3.2 reduce_sum.46
  485.2 83.3 %all-to-all-done = f32[4,256,1024]{2,1,0:T(8,128)} async-done(((f32[4,256,1024]{2,1,0:T(8,128)}), f32[4,256,1024]{2,1,0:T(8,128)}, u32[]{:S(2)}, u32[]{:S(2)}) %all-to-all-start) | async-done | bytes 4194336 | tf_op jit(solution)/shard_map/all_to_all | solution.py:111
  568.5 5.2 copy.69
  573.7 3.2 reduce_sum.45
  578.0 15.0 %fusion.36 = f32[1024,4096]{1,0:T(8,128)} fusion(bf16[1,1024,4096]{2,1,0:T(8,128)(2,1)} %all-gather.4.cloned.1.call-done, bf16[1,1024,1024]{2,1,0:T(8,128)(2,1)S(1)} %copy-done), kind=kOutput, calls=%fused_computation.45 | convolution fusion | flops 8589934592 | bytes 27262976 | tf_op jit(solution)/shard_map/dot_general | solution.py:29
  593.0 1.9 copy.55
  599.7 385.9 %all-gather.6.cloned.1.call-done = f32[4096,4096]{1,0:T(8,128)} async-done(((f32[1024,4096]{1,0:T(8,128)}), f32[4096,4096]{1,0:T(8,128)}) %all-gather.6.cloned.1.call-update) | async-done | bytes 67108880 | tf_op jit(solution)/shard_map/all_gather | solution.py:33
  985.6 27.9 %reduce_sum.47 = f32[1024,4096]{1,0:T(8,128)} reduce(f32[4,1024,4096]{2,1,0:T(8,128)} %bitcast.21, f32[]{:T(128)} %constant.90.clone.1), dimensions={0}, to_apply=%region_10.11 | reduce | flops 12582912 | bytes 83886080 | tf_op jit(solution)/shard_map/reduce_sum | solution.py:33
  (94 shorter events, 29.3 us)
Async XLA Ops:
  7.2 169.9 %copy-start = (bf16[1,1024,1024]{2,1,0:T(8,128)(2,1)S(1)}, bf16[1,1024,1024]{2,1,0:T(8,128)(2,1)}, u32[]{:S(2)}) copy-start(bf16[1,1024,1024]{2,1,0:T(8,128)(2,1)} %param.11) | copy-start | bytes 6291460
  7.2 154.7 %all-gather.4.cloned.1.call-start = ((), (), s32[]{:S(2)}) async-start(), calls=%async_computation.5 | async-start | bytes 10485760 | tf_op jit(solution)/shard_map/all_gather | solution.py:24
  7.9 221.8 %reduce-scatter.4.cloned.1.call-start = ((), (), s32[]{:S(2)}) async-start(), calls=%async_computation.6 | async-start | bytes 6291456 | tf_op jit(solution)/shard_map/reduce_scatter | solution.py:34
  178.5 2.4 copy-start.1
  180.9 3.6 copy-start.3
  180.9 3.7 copy-start.2
  372.6 98.3 %all-to-all-start.1 = ((f32[4,256,1024]{2,1,0:T(8,128)}), f32[4,256,1024]{2,1,0:T(8,128)}, u32[]{:S(2)}, u32[]{:S(2)}) async-start(f32[4,256,1024]{2,1,0:T(8,128)} %all_to_all.27), calls=%async_computation.3 | async-start | bytes 8388608 | tf_op jit(solution)/shard_map/all_to_all | solution.py:112
  470.8 97.7 %all-to-all-start = ((f32[4,256,1024]{2,1,0:T(8,128)}), f32[4,256,1024]{2,1,0:T(8,128)}, u32[]{:S(2)}, u32[]{:S(2)}) async-start(f32[4,256,1024]{2,1,0:T(8,128)} %all_to_all.24), calls=%async_computation.1 | async-start | bytes 8388608 | tf_op jit(solution)/shard_map/all_to_all | solution.py:111
  475.8 120.4 %reduce-scatter.8.cloned.1.call-start = ((), (), s32[]{:S(2)}) async-start(), calls=%async_computation.8 | async-start | bytes 786432 | tf_op jit(solution)/shard_map/reduce_scatter | solution.py:116
  485.1 112.8 %reduce-scatter.6.cloned.1.call-start = ((), (), s32[]{:S(2)}) async-start(), calls=%async_computation.7 | async-start | bytes 786432 | tf_op jit(solution)/shard_map/reduce_scatter | solution.py:115
  578.0 407.7 %all-gather.6.cloned.1.call-start = ((), (), s32[]{:S(2)}) async-start(), calls=%async_computation.9 | async-start | bytes 83886080 | tf_op jit(solution)/shard_map/all_gather | solution.py:33
Sparse Core Ops, SparseCore 0:
  9.6 152.3 all-gather.3
  177.1 52.5 reduce-scatter.3
  485.3 15.0 reduce-scatter.7
  578.1 12.7 reduce-scatter.5
  593.1 392.4 all-gather.5
